TPU v7x, 256 devices: a whole 4x4x8 slice. The times are simulated.
256 devices in a mesh: grp: 4 (over z_lo), dp: 64 (over z_hi, x, y, core).
Axes of the slice: x: 4, y: 4, z: 8 (z_hi: 2, z_lo: 4; z = z_hi * 4 + z_lo), core: 2. Of those that a mesh axis runs over, the one named last changes fastest.
Arguments:
- grads: bfloat16 [4, 64, 64, 8192], P('grp', 'dp'), may hold values from -12 to 12
- momentum: float32 [4, 64, 64, 8192], P('grp', 'dp'), may hold values from -152 to 152
- worker_error: float32 [4, 64, 64, 8192], P('grp', 'dp'), may hold values from -6 to 6
- server_error: float32 [4, 64, 8192], P('grp', 'dp'), may hold values from -2 to 2
Outputs:
- synced: float32 [64, 8192], replicated
- worker_error_out: float32 [4, 64, 64, 8192], P('grp', 'dp')
- server_error_out: float32 [4, 64, 8192], P('grp', 'dp')
All inputs are finite; a program needn't handle non-finite values.
Results may differ from a plain program's by a relative error of at most 0.012.
Values may be sent and summed in bfloat16 or wider, within the bound.
No kernel may reach another device: no remote copies, remote signals or barrier semaphores. Data moves between devices by JAX's collectives and lax.ppermute only.
A program may use at most 64 MiB of HBM per device.

v0:
```python
import jax
import jax.numpy as jnp
from jax import lax
from jax.sharding import Mesh
from jax.sharding import PartitionSpec as P

DP = ("dp_0", "dp_1", "dp_2", "dp_3")


def sent_together(arrays, axis, split_dim, concat_dim, along):
    columns = [a.reshape(*a.shape[:along], -1) for a in arrays]
    both = jnp.concatenate(columns, axis=along)
    result, at, done = (
        lax.all_to_all(both, axis, split_axis=split_dim, concat_axis=concat_dim, tiled=True),
        0,
        [],
    )
    for a, column in zip(arrays, columns):
        slab = result[..., at : at + column.shape[along]]
        done.append(slab.reshape(*slab.shape[:along], *a.shape[along:]))
        at += column.shape[along]
    return tuple(done)


def from_everyone(x, axis):
    copies = jnp.broadcast_to(x, (lax.axis_size(axis), *x.shape))
    return lax.all_to_all(copies, axis, split_axis=0, concat_axis=0, tiled=True)


def taken_together(x, axis):
    return from_everyone(x, axis).astype(jnp.float32).sum(axis=0)


def in_order(blocks, dim):
    blocks = jnp.moveaxis(blocks, 0, dim)
    shape = blocks.shape
    return blocks.reshape(*shape[:dim], shape[dim] * shape[dim + 1], *shape[dim + 2 :])


def whole_of(x, axes, dim):
    far, near = axes
    blocks = from_everyone(from_everyone(x, far), near)
    return in_order(blocks.swapaxes(0, 1).reshape(-1, *x.shape), dim)


def compress(values):
    row_scale = (jnp.mean(jnp.abs(values), axis=-1) + 1e-06).astype(jnp.bfloat16)
    scale_wide = row_scale.astype(jnp.float32)[..., None]
    coded = jnp.tanh(values / scale_wide).astype(jnp.bfloat16)
    leftover = values - scale_wide * coded.astype(jnp.float32)
    return (row_scale, coded, leftover)


def per_device(grads, momentum, worker_error, server_error):
    blended = 0.9 * momentum + 0.1 * grads.astype(jnp.float32) + worker_error
    row_scale, coded, werr_new = compress(blended)
    got_code, got_scale = sent_together((coded, row_scale), DP, 2, 1, 3)
    workers = lax.axis_size(DP)
    groups = lax.axis_size("grp")
    summed = jnp.einsum("gwrd,gwr->grd", got_code, got_scale, preferred_element_type=jnp.float32)
    server_input = summed / workers + server_error
    server_scale, server_code, serr_new = compress(server_input)
    decoded = server_scale.astype(jnp.float32)[..., None] * server_code.astype(jnp.float32)
    averaged = taken_together(decoded.astype(jnp.bfloat16), "grp").astype(jnp.float32) / groups
    synced = whole_of(averaged.astype(jnp.bfloat16), (("dp_0", "dp_1", "dp_2"), "dp_3"), 1).astype(
        averaged.dtype
    )[0]
    return (synced, werr_new, serr_new)


def solution(mesh):
    torus = Mesh(
        mesh.devices.reshape(mesh.shape["grp"], 2, 4, 4, 2), ("grp", "dp_0", "dp_1", "dp_2", "dp_3")
    )
    return jax.shard_map(
        per_device,
        mesh=torus,
        in_specs=(
            P("grp", DP, None, None),
            P("grp", DP, None, None),
            P("grp", DP, None, None),
            P("grp", DP, None),
        ),
        out_specs=(P(), P("grp", DP, None, None), P("grp", DP, None)),
        check_vma=False,
    )
```

profile of v0, /device:TPU:1, one launch (start us, length us, event | category | flops | bytes accessed | tf_op | source)
XLA Modules:
  0.0 127.1 jit_solution(12845517313858532942)
XLA Ops:
  0.6 3.1 %abs_reduce_fusion = (f32[64]{0:T(128)S(1)}, f32[1,1,64,8192]{3,2,1,0:T(8,128)S(1)}) fusion(f32[1,1,64,8192]{3,2,1,0:T(8,128)} %param.6, bf16[1,1,64,8192]{3,2,1,0:T(8,128)(2,1)} %param.4, f32[1,1,64,8192]{3,2,1,0:T(8,128)} %param.5), kind=kLoop, calls=%fused_computation.3 | loop fusion | flops 3669952 | bytes 7340288 | tf_op jit(solution)/shard_map/reduce_sum | solution.py:47
  3.8 0.1 copy.40
  3.9 1.8 %multiply_subtract_fusion = (f32[1,1,64,8192]{3,2,1,0:T(8,128)}, bf16[1,1,64,8192]{3,2,1,0:T(8,128)(2,1)S(1)}) fusion(f32[1,1,64,8192]{3,2,1,0:T(8,128)S(1)} %get-tuple-element.20, f32[64]{0:T(128)S(1)} %get-tuple-element.23), kind=kLoop, calls=%fused_computation.1 | loop fusion | flops 2621440 | bytes 5243136 | tf_op jit(solution)/shard_map/sub | solution.py:50
  5.6 0.1 pad_maximum_fusion
  5.7 1.6 %copy.41 = bf16[1,1,64,8193]{3,1,0,2:T(2,128)(2,1)S(1)} copy(bf16[1,1,64,8193]{3,2,1,0:T(8,128)(2,1)S(1)} %pad_maximum_fusion) | data formatting | bytes 2097408 | tf_op jit(solution)/shard_map/concatenate | solution.py:12
  7.4 71.3 %all_to_all.30 = bf16[1,1,64,8193]{3,1,0,2:T(2,128)(2,1)S(1)} all-to-all(bf16[1,1,64,8193]{3,1,0,2:T(2,128)(2,1)S(1)} %copy.41), channel_id=1, replica_groups=mesh['grp'=4,'dp_0'=2,'dp_1'=4,'dp_2'=4,'dp_3'=2] {'dp_0','dp_1','dp_2',..., dimensions={2} | all-to-all | bytes 2097408 | tf_op jit(solution)/shard_map/all_to_all | solution.py:14
  78.7 0.0 copy-start
  78.7 0.1 copy.49
  78.8 0.1 slice_reduce_fusion
  78.9 0.2 fusion
  79.2 0.3 copy-done
  79.5 0.7 abs_reduce_fusion.1
  80.8 0.7 fusion.2
  81.5 0.1 convert_reduce_fusion.1
  81.6 0.1 broadcast_in_dim.12
  81.6 0.5 broadcast.45
  82.1 1.0 reduce.7
  83.2 0.1 reshape.85
  83.3 7.4 %all_to_all.31 = bf16[4,2,4096]{2,1,0:T(2,128)(2,1)S(1)} all-to-all(bf16[4,2,4096]{2,1,0:T(2,128)(2,1)S(1)} %reshape.85), channel_id=1, replica_groups=mesh['grp'=4,'dp_0'=2,'dp_1'=4,'dp_2'=4,'dp_3'=2] {'grp'}, dimensions={0} | all-to-all | bytes 131072 | tf_op jit(solution)/shard_map/all_to_all | solution.py:27
  90.6 0.1 reshape.86
  90.7 0.1 convert_reduce_fusion
  90.8 0.9 broadcast_in_dim.13
  91.8 3.8 %reduce.8 = bf16[32,8192]{1,0:T(8,128)(2,1)S(1)} reduce(bf16[32,1,1,8192]{3,2,1,0:T(2,128)(2,1)S(1)} %broadcast_in_dim.13, bf16[]{:T(256)} %broadcast.45), dimensions={1,2}, to_apply=%broadcast_in_dim.13.reduce_sub_computation | reduce | bytes 1048578 | tf_op jit(solution)/shard_map/broadcast_in_dim | solution.py:26
  95.6 0.4 reshape.87
  96.0 16.5 %all_to_all.32 = bf16[32,2,4096]{2,1,0:T(2,128)(2,1)S(1)} all-to-all(bf16[32,2,4096]{2,1,0:T(2,128)(2,1)S(1)} %reshape.87), channel_id=1, replica_groups=mesh['grp'=4,'dp_0'=2,'dp_1'=4,'dp_2'=4,'dp_3'=2] {'dp_0','dp_1','dp_2'}, dimensions={0} | all-to-all | bytes 1048576 | tf_op jit(solution)/shard_map/all_to_all | solution.py:27
  112.5 0.5 reshape.88
  113.0 0.6 copy.50
  113.6 0.1 broadcast_in_dim.14
  113.7 9.2 %all_to_all.33 = bf16[2,32,1,1,8192]{4,1,3,2,0:T(8,128)(2,1)S(1)} all-to-all(bf16[2,32,1,1,8192]{4,1,3,2,0:T(8,128)(2,1)S(1)} %broadcast_in_dim.14), channel_id=1, replica_groups=mesh['grp'=4,'dp_0'=2,'dp_1'=4,'dp_2'=4,'dp_3'=2] {'dp_3'}, dimensions={0} | all-to-all | bytes 2097152 | tf_op jit(solution)/shard_map/all_to_all | solution.py:27
  122.9 0.1 convert_bitcast_fusion
  123.1 1.6 %copy.43 = f32[32,2,1,1,8192]{4,1,0,3,2:T(2,128)S(1)} copy(f32[32,2,1,1,8192]{4,0,3,2,1:T(8,128)S(1)} %convert_bitcast_fusion) | data formatting | bytes 4194304 | tf_op jit(solution)/shard_map/convert_element_type | solution.py:65
  124.7 2.4 %reshape.79 = f32[64,8192]{1,0:T(8,128)} reshape(f32[32,2,1,1,8192]{4,1,0,3,2:T(2,128)S(1)} %copy.43) | data formatting | bytes 4194304 | tf_op jit(solution)/shard_map/convert_element_type | solution.py:65
  (3 shorter events, 0.0 us)
Async XLA Ops:
  78.7 0.8 copy-start
where the time goes:
time: 129 us; the launch traced here: 127 us
  blocking collectives  104 us (81%)
  other arithmetic  11.4 us (9%)
  local copies, waits for them, and re-layouts  9.62 us (7%)
  between operations  1.41 us (1%)
    all_to_all x1, blocking collectives, sent_together(): lax.all_to_all(both, axis, split_axis=split_dim, concat_axis=concat_dim,...  71.3 us
    all_to_all x3, blocking collectives, from_everyone(): return lax.all_to_all(copies, axis, split_axis=0, concat_axis=0, tiled=True)  33.1 us
    broadcast_in_dim x2, other arithmetic, from_everyone(): copies = jnp.broadcast_to(x, (lax.axis_size(axis), *x.shape))  4.84 us
    convert_element_type x2, local copies, waits for them, and re-layouts, per_device(): whole_of(averaged.astype(jnp.bfloat16), (('dp_0', 'dp_1', 'dp_2'), 'dp_3'...  4.06 us
    reduce_sum x2, other arithmetic, compress(): jnp.mean(jnp.abs(values), axis=-1) + 1e-06  3.8 us

commit v1 on v0

v1 whole, which is shorter than its diff:
```python
import functools

import jax
import jax.numpy as jnp
from jax import lax
from jax.experimental import pallas as pl
from jax.experimental.pallas import tpu as pltpu
from jax.sharding import Mesh
from jax.sharding import PartitionSpec as P

DP = ("zh", "x", "y", "core")
F32, BF16 = jnp.float32, jnp.bfloat16
LANES, SUB = 128, 8
EPS = 1e-6


def blend(m, g, e):
    return 0.9 * m + 0.1 * g.astype(F32) + e


def row_scale(total, width):
    return (total * (1.0 / width) + EPS).astype(BF16).astype(F32)


def encode_kernel(core_ref, g_ref, m_ref, e_ref, theirs_ref, mine_ref, scale_ref, tile):
    width = m_ref.shape[1]
    cols = width // LANES
    total = jnp.zeros((SUB, LANES), F32)
    for j in range(cols):
        at = pl.ds(j * LANES, LANES)
        b = blend(m_ref[:, at], g_ref[:, at], e_ref[:, at])
        tile[pl.ds(j * SUB, SUB), :] = b
        total = total + jnp.abs(b)
    scale = row_scale(jnp.sum(total, axis=1, keepdims=True), width)
    wide = jnp.broadcast_to(scale, (SUB, LANES))
    inverse = jnp.broadcast_to(1.0 / scale, (SUB, LANES))
    scale_ref[...] = wide
    for j in range(cols):
        at = pl.ds(j * SUB, SUB)
        code = jnp.tanh(tile[at, :] * inverse).astype(BF16).astype(F32)
        tile[at, :] = wide * code
    core = core_ref[0]
    for i in range(SUB // 2):
        for q in range(cols // SUB):
            to = pl.ds(q * SUB, SUB)
            base = q * SUB * SUB + 2 * i
            mine_ref[i, to, :] = tile[pl.ds(base + core, SUB, stride=SUB), :]
            theirs_ref[i, to, :] = tile[pl.ds(base + 1 - core, SUB, stride=SUB), :].astype(BF16)


def encode(core, g, m, e):
    rows, width = m.shape
    cols = width // LANES
    block = pl.BlockSpec((SUB, width), lambda i, c: (i, 0))
    half = pl.BlockSpec((SUB // 2, cols, LANES), lambda i, c: (i, 0, 0))
    return pl.pallas_call(
        encode_kernel,
        grid_spec=pltpu.PrefetchScalarGridSpec(
            num_scalar_prefetch=1,
            grid=(rows // SUB,),
            in_specs=[block, block, block],
            out_specs=[half, half, pl.BlockSpec((SUB, LANES), lambda i, c: (i, 0))],
            scratch_shapes=[pltpu.VMEM((cols * SUB, LANES), F32)],
        ),
        out_shape=[
            jax.ShapeDtypeStruct((rows // 2, cols, LANES), BF16),
            jax.ShapeDtypeStruct((rows // 2, cols, LANES), F32),
            jax.ShapeDtypeStruct((rows, LANES), F32),
        ],
        name="encode",
    )(core, g, m, e)


def leftover_kernel(g_ref, m_ref, e_ref, scale_ref, out_ref):
    wide = scale_ref[...]
    inverse = 1.0 / wide
    for j in range(m_ref.shape[1] // LANES):
        at = pl.ds(j * LANES, LANES)
        b = blend(m_ref[:, at], g_ref[:, at], e_ref[:, at])
        code = jnp.tanh(b * inverse).astype(BF16).astype(F32)
        out_ref[:, at] = b - wide * code


def leftover(g, m, e, scale):
    rows, width = m.shape
    block = pl.BlockSpec((SUB, width), lambda i: (i, 0))
    return pl.pallas_call(
        leftover_kernel,
        grid=(rows // SUB,),
        in_specs=[block, block, block, pl.BlockSpec((SUB, LANES), lambda i: (i, 0))],
        out_specs=block,
        out_shape=jax.ShapeDtypeStruct((rows, width), F32),
        name="leftover",
    )(g, m, e, scale)


def pair_kernel(a_ref, b_ref, out_ref):
    out_ref[...] = (a_ref[...] + b_ref[...].astype(F32)).astype(BF16)


def pair_sum(a, b):
    return pl.pallas_call(
        pair_kernel, out_shape=jax.ShapeDtypeStruct(a.shape, BF16), name="pair_sum"
    )(a, b)


def server_kernel(workers, got_ref, e_ref, copies_ref, out_ref):
    total = got_ref[0].astype(F32)
    for k in range(1, got_ref.shape[0]):
        total = total + got_ref[k].astype(F32)
    x = total * (1.0 / workers) + e_ref[...]
    scale = row_scale(jnp.sum(jnp.abs(x), keepdims=True), x.size)
    code = jnp.tanh(x / scale).astype(BF16).astype(F32)
    decoded = scale * code
    out_ref[...] = x - decoded
    sent = decoded.astype(BF16)
    for k in range(copies_ref.shape[0]):
        copies_ref[k] = sent


def server(got, e, workers, copies):
    return pl.pallas_call(
        functools.partial(server_kernel, workers),
        out_shape=[
            jax.ShapeDtypeStruct((copies, *e.shape), BF16),
            jax.ShapeDtypeStruct(e.shape, F32),
        ],
        name="server",
    )(got, e)


def average_kernel(got_ref, out_ref):
    groups, halves = got_ref.shape[0], got_ref.shape[1]
    for h in range(halves):
        total = got_ref[0, h].astype(F32)
        for k in range(1, groups):
            total = total + got_ref[k, h].astype(F32)
        sent = (total * (1.0 / groups)).astype(BF16)
        for k in range(out_ref.shape[0]):
            out_ref[k, h] = sent


def average(got, copies):
    return pl.pallas_call(
        average_kernel,
        out_shape=jax.ShapeDtypeStruct((copies, *got.shape[1:]), BF16),
        name="average",
    )(got)


def assemble_kernel(core_ref, mine_ref, theirs_ref, out_ref, tile):
    core = core_ref[0]
    cols = out_ref.shape[1] // LANES
    for i in range(SUB // 2):
        for q in range(cols // SUB):
            at = pl.ds(q * SUB, SUB)
            base = q * SUB * SUB + 2 * i
            tile[pl.ds(base + core, SUB, stride=SUB), :] = mine_ref[0, i, 0, at, :].astype(F32)
            tile[pl.ds(base + 1 - core, SUB, stride=SUB), :] = theirs_ref[0, i, 0, at, :].astype(F32)
    for j in range(cols):
        out_ref[:, pl.ds(j * LANES, LANES)] = tile[pl.ds(j * SUB, SUB), :]


def assemble(core, mine, theirs):
    xs, ys, zs, cols, _ = mine.shape
    assert ys * 2 == SUB
    rows, width = xs * ys * zs * 2, cols * LANES
    part = pl.BlockSpec((1, ys, 1, cols, LANES), lambda i, c: (i % xs, 0, i // xs, 0, 0))
    return pl.pallas_call(
        assemble_kernel,
        grid_spec=pltpu.PrefetchScalarGridSpec(
            num_scalar_prefetch=1,
            grid=(rows // SUB,),
            in_specs=[part, part],
            out_specs=pl.BlockSpec((SUB, width), lambda i, c: (i, 0)),
            scratch_shapes=[pltpu.VMEM((cols * SUB, LANES), F32)],
        ),
        out_shape=jax.ShapeDtypeStruct((rows, width), F32),
        name="assemble",
    )(core, mine, theirs)


def everyone(x, axes):
    return lax.all_to_all(x, axes, split_axis=0, concat_axis=0, tiled=True)


def swapped(x):
    return lax.ppermute(x, "core", [(0, 1), (1, 0)])


def per_device(grads, momentum, worker_error, server_error):
    g, m, e = (a[0, 0] for a in (grads, momentum, worker_error))
    width = m.shape[1]
    cols = width // LANES
    zs, xs, ys = (lax.axis_size(n) for n in ("zh", "x", "y"))
    groups, workers = lax.axis_size("grp"), lax.axis_size(DP)
    core = lax.axis_index("core").astype(jnp.int32)[None]
    theirs, mine, scale = encode(core, g, m, e)
    partial = pair_sum(mine, swapped(theirs))
    got = everyone(partial, ("zh", "x", "y"))
    werr = leftover(g, m, e, scale)
    copies, serr = server(got, server_error.reshape(cols, LANES), workers, groups * zs)
    rows = everyone(copies, ("grp", "zh")).reshape(groups, zs, cols, LANES)
    spread = average(rows, xs * ys)
    own = everyone(spread, ("x", "y")).reshape(xs, ys, zs, cols, LANES)
    synced = assemble(core, own, swapped(own))
    return (synced, werr[None, None], serr.reshape(1, 1, width))


def solution(mesh):
    torus = Mesh(
        mesh.devices.reshape(mesh.shape["grp"], 2, 4, 4, 2), ("grp", "zh", "x", "y", "core")
    )
    return jax.shard_map(
        per_device,
        mesh=torus,
        in_specs=(
            P("grp", DP, None, None),
            P("grp", DP, None, None),
            P("grp", DP, None, None),
            P("grp", DP, None),
        ),
        out_specs=(P(), P("grp", DP, None, None), P("grp", DP, None)),
        check_vma=False,
    )
```

time: 129 us -> 91.9 us (0.71)
  blocking collectives: 104 us -> 54 us
  Pallas kernels: 0 us -> 24.8 us
  other arithmetic: 11.4 us -> 0 us
  starting transfers between devices: 0 us -> 8.05 us
  local copies, waits for them, and re-layouts: 9.62 us -> 1.58 us
  waiting for transfers between devices: 0 us -> 1.75 us
    all_to_all x4 -> x3, blocking collectives: 104 us -> 54 us  [everyone(): return lax.all_to_all(x, axes, split_axis=0, concat_axis=0, tiled=True)]
    pallas_call x0 -> x6, Pallas kernels: none -> 24.8 us  [the longest x1 6.92 us: encode(): pl.pallas_call(encode_kernel, grid_spec=pltpu.PrefetchScalarGridSpec(num_...]
    ppermute x0 -> x2, starting transfers between devices: none -> 8.05 us  [swapped(): return lax.ppermute(x, 'core', [(0, 1), (1, 0)])]
    broadcast_in_dim x2 -> x0, other arithmetic: 4.84 us -> none  [from_everyone(): copies = jnp.broadcast_to(x, (lax.axis_size(axis), *x.shape))]
    convert_element_type x4 -> x0, local copies, waits for them, and re-layouts: 4.27 us -> none  [the longest x2 4.06 us: per_device(): whole_of(averaged.astype(jnp.bfloat16), (('dp_0', 'dp_1', 'dp_2'), 'dp_3'...]
    reduce_sum x3 -> x0, other arithmetic: 3.94 us -> none  [the longest x2 3.8 us: compress(): jnp.mean(jnp.abs(values), axis=-1) + 1e-06]
    sub x2 -> x0, other arithmetic: 2.43 us -> none  [compress(): leftover = values - scale_wide * coded.astype(jnp.float32)]
    ppermute x0 -> x2, waiting for transfers between devices: none -> 1.75 us  [swapped(): return lax.ppermute(x, 'core', [(0, 1), (1, 0)])]
  transfers between devices with their start and end apart: 0 -> 2, of which waited for: 0 -> 1; matrix products, arithmetic and copies ran while one was open for 0% -> 0% of each run, Pallas kernels for 0% -> 7%
where the time goes in v1:
time: 91.9 us; the launch traced here: 90.8 us
  blocking collectives  54 us (59%)
  Pallas kernels  24.8 us (27%)
  starting transfers between devices  8.05 us (9%)
  waiting for transfers between devices  1.75 us (2%)
  local copies, waits for them, and re-layouts  1.58 us (2%)
    all_to_all x3, blocking collectives, everyone(): return lax.all_to_all(x, axes, split_axis=0, concat_axis=0, tiled=True)  54 us
    ppermute x2, starting transfers between devices, swapped(): return lax.ppermute(x, 'core', [(0, 1), (1, 0)])  8.05 us
    pallas_call x1, Pallas kernels, encode(): pl.pallas_call(encode_kernel, grid_spec=pltpu.PrefetchScalarGridSpec(num_...  6.92 us
    pallas_call x1, Pallas kernels, leftover(): pl.pallas_call(leftover_kernel, grid=(rows // SUB,), in_specs=[block, blo...  6.54 us
    pallas_call x1, Pallas kernels, assemble(): pl.pallas_call(assemble_kernel, grid_spec=pltpu.PrefetchScalarGridSpec(nu...  5.44 us
    pallas_call x1, Pallas kernels, pair_sum(): pl.pallas_call(pair_kernel, out_shape=jax.ShapeDtypeStruct(a.shape, BF16)...  2.24 us
    pallas_call x1, Pallas kernels, server(): pl.pallas_call(functools.partial(server_kernel, workers), out_shape=[jax....  1.94 us
  transfers between devices with their start and end apart: 2, of which 1 were waited for; matrix products, arithmetic and copies ran while one was open for 0% of the time, Pallas kernels for 7%

profile of v1, /device:TPU:1, one launch (start us, length us, event | category | flops | bytes accessed | tf_op | source)
XLA Modules:
  0.0 90.8 jit_solution(12173920708918715087)
XLA Ops:
  0.6 6.9 %encode.1 = (bf16[32,64,128]{2,1,0:T(8,128)(2,1)}, f32[32,64,128]{2,1,0:T(8,128)}, f32[64,128]{1,0:T(8,128)}) custom-call(s32[1]{0:T(128)} %bitcast.core_ref, bf16[64,8192]{1,0:T(8,128)(2,1)} %bitcast.13, f32[64,8192]{1,0:T(8,128)} %bitcast.9, f32[64,8192]{1,0:T(8,128)} %bitcast.11), custom_call_target="tpu_custom_call" | custom-call | tf_op jit(solution)/shard_map/encode/pallas_call | solution.py:56
  7.6 3.2 %collective-permute-start = (bf16[32,64,128]{2,1,0:T(8,128)(2,1)}, bf16[32,64,128]{2,1,0:T(8,128)(2,1)S(1)}, u32[]{:S(2)}, u32[]{:S(2)}) collective-permute-start(bf16[32,64,128]{2,1,0:T(8,128)(2,1)} %get-tuple-element.9), channel_id=1, source_target_pairs={{0,1},{1,0},{2,3},{3,2},{4,5},{5,4},{6,7},{7,6},{8,9},{9,8},{10,11... | collective-permute-start | bytes 1572872 | tf_op jit(solution)/shard_map/ppermute | solution.py:188
  10.8 1.7 %collective-permute-done.b_ref = bf16[32,64,128]{2,1,0:T(8,128)(2,1)S(1)} collective-permute-done((bf16[32,64,128]{2,1,0:T(8,128)(2,1)}, bf16[32,64,128]{2,1,0:T(8,128)(2,1)S(1)}, u32[]{:S(2)}, u32[]{:S(2)}) %collective-permute-start) | collective-permute-done | bytes 524320 | tf_op jit(solution)/shard_map/ppermute | solution.py:188
  12.5 0.0 copy-start.2
  12.5 0.8 copy-done.2
  13.3 2.2 %pair_sum.1 = bf16[32,64,128]{2,1,0:T(8,128)(2,1)} custom-call(f32[32,64,128]{2,1,0:T(8,128)} %get-tuple-element.8.a_ref, bf16[32,64,128]{2,1,0:T(8,128)(2,1)} %copy-done.2), custom_call_target="tpu_custom_call" | custom-call | tf_op jit(solution)/shard_map/pair_sum/pallas_call | solution.py:102
  15.5 26.7 %all_to_all.15.got_ref = bf16[32,64,128]{2,1,0:T(8,128)(2,1)} all-to-all(bf16[32,64,128]{2,1,0:T(8,128)(2,1)} %pair_sum.1), channel_id=1, replica_groups=mesh['grp'=4,'zh'=2,'x'=4,'y'=4,'core'=2] {'zh','x','y'}, dimensions={0} | all-to-all | bytes 1048576 | tf_op jit(solution)/shard_map/all_to_all | solution.py:184
  42.2 1.9 %server.1 = (bf16[8,64,128]{2,1,0:T(8,128)(2,1)}, f32[64,128]{1,0:T(8,128)}) custom-call(bf16[32,64,128]{2,1,0:T(8,128)(2,1)} %all_to_all.15.got_ref, f32[64,128]{1,0:T(8,128)} %bitcast.19), custom_call_target="tpu_custom_call" | custom-call | tf_op jit(solution)/shard_map/server/pallas_call | solution.py:122
  44.1 14.4 %all_to_all.16 = bf16[8,64,128]{2,1,0:T(8,128)(2,1)} all-to-all(bf16[8,64,128]{2,1,0:T(8,128)(2,1)} %get-tuple-element.10), channel_id=1, replica_groups=mesh['grp'=4,'zh'=2,'x'=4,'y'=4,'core'=2] {'grp','zh'}, dimensions={0} | all-to-all | bytes 262144 | tf_op jit(solution)/shard_map/all_to_all | solution.py:184
  58.5 1.8 %average.1 = bf16[16,2,64,128]{3,2,1,0:T(8,128)(2,1)} custom-call(bf16[4,2,64,128]{3,2,1,0:T(8,128)(2,1)} %bitcast.18), custom_call_target="tpu_custom_call" | custom-call | tf_op jit(solution)/shard_map/average/pallas_call | solution.py:144
  60.3 12.9 %all_to_all.17 = bf16[16,2,64,128]{3,2,1,0:T(8,128)(2,1)S(1)} all-to-all(bf16[16,2,64,128]{3,2,1,0:T(8,128)(2,1)} %average.1), channel_id=1, replica_groups=mesh['grp'=4,'zh'=2,'x'=4,'y'=4,'core'=2] {'x','y'}, dimensions={0} | all-to-all | bytes 1048576 | tf_op jit(solution)/shard_map/all_to_all | solution.py:184
  73.2 0.0 copy-start
  73.2 4.8 %collective-permute-start.1 = (bf16[4,4,2,64,128]{4,3,2,1,0:T(8,128)(2,1)S(1)}, bf16[4,4,2,64,128]{4,3,2,1,0:T(8,128)(2,1)S(1)}, u32[]{:S(2)}, u32[]{:S(2)}) collective-permute-start(bf16[4,4,2,64,128]{4,3,2,1,0:T(8,128)(2,1)S(1)} %bitcast.16), channel_id=1, source_target_pairs={{0,1},{1,0},{2,3},{3,2},{4,5},{5,4},{6,7},{7,6},{8,9},{9,8},{10,11... | collective-permute-start | bytes 1572872 | tf_op jit(solution)/shard_map/ppermute | solution.py:188
  78.1 6.5 %leftover.1 = f32[64,8192]{1,0:T(8,128)} custom-call(bf16[64,8192]{1,0:T(8,128)(2,1)} %bitcast.14, f32[64,8192]{1,0:T(8,128)} %bitcast.10, f32[64,8192]{1,0:T(8,128)} %bitcast.12, f32[64,128]{1,0:T(8,128)} %get-tuple-element.11.scale_ref), custom_call_target="tpu_custom_call" | custom-call | tf_op jit(solution)/shard_map/leftover/pallas_call | solution.py:87
  84.6 0.0 copy-done
  84.6 0.0 collective-permute-done.1.theirs_ref
  84.6 0.0 copy-start.1
  84.6 0.8 copy-done.1
  85.4 5.4 %assemble.1 = f32[64,8192]{1,0:T(8,128)} custom-call(s32[1]{0:T(128)} %bitcast.core_ref, bf16[4,4,2,64,128]{4,3,2,1,0:T(8,128)(2,1)} %bitcast.17, bf16[4,4,2,64,128]{4,3,2,1,0:T(8,128)(2,1)} %copy-done.1), custom_call_target="tpu_custom_call" | custom-call | tf_op jit(solution)/shard_map/assemble/pallas_call | solution.py:169
Async XLA Ops:
  7.6 4.9 %collective-permute-start = (bf16[32,64,128]{2,1,0:T(8,128)(2,1)}, bf16[32,64,128]{2,1,0:T(8,128)(2,1)S(1)}, u32[]{:S(2)}, u32[]{:S(2)}) collective-permute-start(bf16[32,64,128]{2,1,0:T(8,128)(2,1)} %get-tuple-element.9), channel_id=1, source_target_pairs={{0,1},{1,0},{2,3},{3,2},{4,5},{5,4},{6,7},{7,6},{8,9},{9,8},{10,11... | collective-permute-start | bytes 1572872 | tf_op jit(solution)/shard_map/ppermute | solution.py:188
  12.5 0.8 copy-start.2
  73.2 11.4 %copy-start = (bf16[16,2,64,128]{3,2,1,0:T(8,128)(2,1)}, bf16[16,2,64,128]{3,2,1,0:T(8,128)(2,1)S(1)}, u32[]{:S(2)}) copy-start(bf16[16,2,64,128]{3,2,1,0:T(8,128)(2,1)S(1)} %all_to_all.17) | copy-start | bytes 1572868
  73.2 11.4 %collective-permute-start.1 = (bf16[4,4,2,64,128]{4,3,2,1,0:T(8,128)(2,1)S(1)}, bf16[4,4,2,64,128]{4,3,2,1,0:T(8,128)(2,1)S(1)}, u32[]{:S(2)}, u32[]{:S(2)}) collective-permute-start(bf16[4,4,2,64,128]{4,3,2,1,0:T(8,128)(2,1)S(1)} %bitcast.16), channel_id=1, source_target_pairs={{0,1},{1,0},{2,3},{3,2},{4,5},{5,4},{6,7},{7,6},{8,9},{9,8},{10,11... | collective-permute-start | bytes 1572872 | tf_op jit(solution)/shard_map/ppermute | solution.py:188
  84.6 0.8 copy-start.1
